TPU v7x, 512 devices: a whole 4x8x8 slice. The times are simulated.
512 devices in a mesh: gz: 16 (over y, x_hi), gy: 32 (over z, x_lo, core).
Axes of the slice: x: 4 (x_hi: 2, x_lo: 2; x = x_hi * 2 + x_lo), y: 8, z: 8, core: 2. Of those that a mesh axis runs over, the one named last changes fastest.
Arguments:
- field_b: float32 [3, 2, 2048, 2048], P(None, None, 'gy', 'gz'), may hold values from -6 to 6
- density: float32 [2, 2048, 2048], P(None, 'gy', 'gz'), may hold values from 0.5 to 2
- level_y: int32 [2048], P('gy'), may hold values from 0 to 7
- level_z: int32 [2048], P('gz'), may hold values from 0 to 7
- bins: int32 [1024, 2048], P(('gz', 'gy')), may hold values from 0 to 1023
Outputs:
- emf: bfloat16 [3, 2, 2048, 2048], P(None, None, 'gy', 'gz')
- mode_power: float32 [1024, 2048], P(('gz', 'gy'))
- spectrum: float32 [1024], replicated
All inputs are finite; a program needn't handle non-finite values.
Results may differ from a plain program's by a relative error of at most 0.0035.
Values may be sent and summed in bfloat16 or wider, within the bound.
No kernel may reach another device: no remote copies, remote signals or barrier semaphores. Data moves between devices by JAX's collectives and lax.ppermute only.
A program may use at most 64 MiB of HBM per device.

v0:
```python
import math
import jax
import jax.numpy as jnp
from jax import lax
from jax.sharding import PartitionSpec as P

NY = 2048
NZ = 2048
NB = 1024
KZ = 1024


def extended(cells, sides, width):
    for axis, dim in sides:
        count = lax.axis_size(axis)
        head = lax.slice_in_dim(cells, 0, width, axis=dim)
        tail = lax.slice_in_dim(cells, cells.shape[dim] - width, cells.shape[dim], axis=dim)
        cells = jnp.concatenate(
            [
                lax.ppermute(tail, axis, [(i, (i + 1) % count) for i in range(count)]),
                cells,
                lax.ppermute(head, axis, [((i + 1) % count, i) for i in range(count)]),
            ],
            axis=dim,
        )
    return cells


def metric(level):
    return 1.0 / (1.0 + 0.25 * level.astype(jnp.float32))


def twiddle(positions, modes, length):
    phase = positions[:, None] * modes[None, :] % length
    angle = phase.astype(jnp.float32) * (2.0 * math.pi / length)
    factor = 1.0 / math.sqrt(length)
    return (
        (jnp.cos(angle) * factor).astype(jnp.bfloat16),
        (jnp.sin(angle) * factor).astype(jnp.bfloat16),
    )


def on_device(field_b, density, level_y, level_z, bins):
    planes = field_b.shape[1]
    y_local = field_b.shape[2]
    metric_y = metric(level_y)[None, None, :, None]
    metric_z = metric(level_z)[None, None, None, :]
    padded = extended(field_b, (("gz", 3), ("gy", 2)), 1)
    grad_y = 0.5 * (padded[:, :, 2:, 1:-1] - padded[:, :, :-2, 1:-1]) * metric_y
    grad_z = 0.5 * (padded[:, :, 1:-1, 2:] - padded[:, :, 1:-1, :-2]) * metric_z
    x_padded = jnp.pad(field_b, ((0, 0), (1, 1), (0, 0), (0, 0)))
    grad_x = 0.5 * (x_padded[:, 2:] - x_padded[:, :-2])
    cur_x = grad_y[2] - grad_z[1]
    cur_y = grad_z[0] - grad_x[2]
    cur_z = grad_x[1] - grad_y[0]
    e_x = (cur_y * field_b[2] - cur_z * field_b[1]) / density
    e_y = (cur_z * field_b[0] - cur_x * field_b[2]) / density
    e_z = (cur_x * field_b[1] - cur_y * field_b[0]) / density
    emf = jnp.stack([e_x, e_y, e_z]).astype(jnp.bfloat16)
    kz_dev = KZ // lax.axis_size("gz")
    z_pos = jnp.arange(NZ, dtype=jnp.int32)
    k_start = lax.axis_index("gz") * kz_dev
    z_cos, z_sin = twiddle(z_pos, k_start + jnp.arange(kz_dev, dtype=jnp.int32), NZ)
    table_z = jnp.concatenate([z_cos, -z_sin], axis=1)
    summed = jnp.einsum(
        "cxyz,zk->kcxy",
        lax.all_gather(emf, "gz", axis=3, tiled=True),
        table_z,
        preferred_element_type=jnp.float32,
    )
    z_modes = summed.reshape(2, kz_dev, 3, planes, y_local).astype(jnp.bfloat16)
    spread = lax.all_to_all(z_modes, "gy", split_axis=1, concat_axis=4, tiled=True)
    k_few = spread.shape[1]
    count = k_few * 3 * planes
    lhs_rows = spread.reshape(2 * count, NY)
    y_block = min(512, NY)
    y_pos = jnp.arange(NY, dtype=jnp.int32)

    def power_block(block_id):
        y_cos, y_sin = twiddle(y_pos, block_id * y_block + jnp.arange(y_block, dtype=jnp.int32), NY)
        product = jnp.dot(
            lhs_rows, jnp.concatenate([y_cos, y_sin], axis=1), preferred_element_type=jnp.float32
        )
        re_cos = product[:count, :y_block]
        re_sin = product[:count, y_block:]
        im_cos = product[count:, :y_block]
        im_sin = product[count:, y_block:]
        real_part = re_cos + im_sin
        imag_part = im_cos - re_sin
        power = (real_part * real_part + imag_part * imag_part).reshape(k_few, 3 * planes, y_block)
        return jnp.sum(power, axis=1) / (3 * planes)

    blocks = lax.map(power_block, jnp.arange(NY // y_block, dtype=jnp.int32))
    mode_power = blocks.transpose(1, 0, 2).reshape(k_few, NY)
    local_bins = jax.ops.segment_sum(mode_power.reshape(-1), bins.reshape(-1), num_segments=NB) * (
        NB / (KZ * NY)
    )
    spectrum = lax.psum(local_bins, ("gz", "gy"))
    return (emf, mode_power, spectrum)


def solution(mesh):
    placed = (
        P(None, None, "gy", "gz"),
        P(None, "gy", "gz"),
        P("gy"),
        P("gz"),
        P(("gz", "gy"), None),
    )
    return jax.shard_map(
        on_device,
        mesh=mesh,
        in_specs=placed,
        out_specs=(P(None, None, "gy", "gz"), P(("gz", "gy"), None), P()),
        check_vma=False,
    )
```

profile of v0, /device:TPU:1, one launch (start us, length us, event | category | flops | bytes accessed | tf_op | source)
XLA Modules:
  0.0 355.4 jit_solution(7134544797630249698)
XLA Ops:
  7.2 0.0 copy-start
  7.2 0.0 all-gather.2.cloned.1.call-start
  7.2 1.2 fusion.43
  8.4 8.4 %collective-permute-start = (f32[3,2,64,1]{3,2,1,0:T(8,128)S(1)}, f32[3,2,64,1]{3,2,1,0:T(8,128)S(1)}, u32[]{:S(2)}, u32[]{:S(2)}) collective-permute-start(f32[3,2,64,1]{3,2,1,0:T(8,128)S(1)} %get-tuple-element.98), channel_id=1, source_target_pairs={{32,0},{64,32},{96,64},{128,96},{160,128},{192,160},{224,192},{256... | collective-permute-start | bytes 4616 | tf_op jit(solution)/shard_map/ppermute | solution.py:22
  16.8 1.9 collective-permute-start.1
  18.7 0.7 divide_multiply_fusion
  19.4 1.0 collective-permute-done
  20.4 7.4 %collective-permute-done.1 = f32[3,2,64,1]{3,2,1,0:T(8,128)S(1)} collective-permute-done((f32[3,2,64,1]{3,2,1,0:T(8,128)S(1)}, f32[3,2,64,1]{3,2,1,0:T(8,128)S(1)}, u32[]{:S(2)}, u32[]{:S(2)}) %collective-permute-start.1) | collective-permute-done | bytes 1568 | tf_op jit(solution)/shard_map/ppermute | solution.py:20
  27.8 0.9 pad_maximum_fusion.11
  28.6 3.8 %collective-permute-start.2 = (f32[3,2,1,130]{3,2,1,0:T(1,128)S(1)}, f32[3,2,1,130]{3,2,1,0:T(1,128)S(1)}, u32[]{:S(2)}, u32[]{:S(2)}) collective-permute-start(f32[3,2,1,130]{3,2,1,0:T(1,128)S(1)} %get-tuple-element.95), channel_id=1, source_target_pairs={{1,0},{2,1},{3,2},{4,3},{5,4},{6,5},{7,6},{8,7},{9,8},{10,9},{11,1... | collective-permute-start | bytes 9368 | tf_op jit(solution)/shard_map/ppermute | solution.py:22
  32.4 2.1 collective-permute-start.3
  34.6 0.7 divide_multiply_fusion.1
  35.2 0.0 collective-permute-done.2
  35.2 7.1 %collective-permute-done.3 = f32[3,2,1,130]{3,2,1,0:T(1,128)S(1)} collective-permute-done((f32[3,2,1,130]{3,2,1,0:T(1,128)S(1)}, f32[3,2,1,130]{3,2,1,0:T(1,128)S(1)}, u32[]{:S(2)}, u32[]{:S(2)}) %collective-permute-start.3) | collective-permute-done | bytes 3152 | tf_op jit(solution)/shard_map/ppermute | solution.py:20
  42.3 1.7 fusion.31
  44.0 0.0 copy-done
  44.0 0.0 copy-done.1
  44.0 0.1 fusion.37
  44.1 0.7 pad_maximum_fusion.8
  44.8 0.0 all-gather.2.cloned.1.call-update
  44.8 2.1 fusion.27
  46.9 2.1 multiply_convert_fusion.3
  49.1 75.1 %all-gather.2.cloned.1.call-done = bf16[3,2,64,2048]{3,2,1,0:T(8,128)(2,1)} async-done(((bf16[3,2,64,128]{3,2,1,0:T(8,128)(2,1)}), bf16[3,2,64,2048]{3,2,1,0:T(8,128)(2,1)}) %all-gather.2.cloned.1.call-update) | async-done | bytes 1572880 | tf_op jit(solution)/shard_map/all_gather | solution.py:67
  124.2 2.0 convolution_convert_fusion
  126.1 0.1 convert_element_type.48
  126.3 0.2 copy.23
  126.4 0.8 reshape.73
  127.2 11.8 %all-to-all-start = ((bf16[32,2,768]{2,1,0:T(2,128)(2,1)}), bf16[32,2,768]{2,1,0:T(2,128)(2,1)S(1)}, u32[]{:S(2)}, u32[]{:S(2)}) async-start(bf16[32,2,768]{2,1,0:T(2,128)(2,1)} %reshape.73), calls=%async_computation | async-start | bytes 196608 | tf_op jit(solution)/shard_map/all_to_all | solution.py:72
  139.0 0.0 copy-done.2
  139.0 8.7 %all-to-all-done = bf16[32,2,768]{2,1,0:T(2,128)(2,1)S(1)} async-done(((bf16[32,2,768]{2,1,0:T(2,128)(2,1)}), bf16[32,2,768]{2,1,0:T(2,128)(2,1)S(1)}, u32[]{:S(2)}, u32[]{:S(2)}) %all-to-all-start) | async-done | bytes 98336 | tf_op jit(solution)/shard_map/all_to_all | solution.py:72
  147.8 0.2 reshape.74
  148.0 0.2 reshape.58
  148.3 76.5 %while.13 = (s32[]{:T(128)}, f32[4,2,512]{2,1,0:T(2,128)S(1)}, s32[4]{0:T(128)S(1)}, bf16[24,2048]{1,0:T(8,128)(2,1)S(1)}, s32[]{:T(128)}, /*index=5*/s32[1]{0:T(128)}, f32[]{:T(128)}) while((s32[]{:T(128)}, f32[4,2,512]{2,1,0:T(2,128)S(1)}, s32[4]{0:T(128)S(1)}, bf16[24,2048]{1,0:T(8,128)(2,1)S(1)}, s32[]{:T(128)}, ...), condition=%wide.region_2.3_spmd.clone, body=%wide.region_0.2_spmd.clone.sunk | while | flops 127963648 | bytes 8798321 | solution.py:93
  148.3 0.6 dynamic_slice.9
  149.5 17.1 %multiply_convert_fusion.5 = (bf16[2048,512]{1,0:T(8,128)(2,1)S(1)}, bf16[2048,512]{1,0:T(8,128)(2,1)S(1)}) fusion(s32[512]{0:T(512)S(1)} %iota_add_fusion.3), kind=kLoop, calls=%fused_computation.16.clone.1 | loop fusion | flops 18874368 | bytes 4196352 | tf_op jit(solution)/shard_map/while/body/eval_jaxpr/convert_element_type | solution.py:38
  166.6 0.6 fusion.52
  167.4 0.6 dynamic_slice.9
  168.6 17.1 %multiply_convert_fusion.5 = (bf16[2048,512]{1,0:T(8,128)(2,1)S(1)}, bf16[2048,512]{1,0:T(8,128)(2,1)S(1)}) fusion(s32[512]{0:T(512)S(1)} %iota_add_fusion.3), kind=kLoop, calls=%fused_computation.16.clone.1 | loop fusion | flops 18874368 | bytes 4196352 | tf_op jit(solution)/shard_map/while/body/eval_jaxpr/convert_element_type | solution.py:38
  185.8 0.6 fusion.52
  186.5 0.6 dynamic_slice.9
  187.8 17.1 %multiply_convert_fusion.5 = (bf16[2048,512]{1,0:T(8,128)(2,1)S(1)}, bf16[2048,512]{1,0:T(8,128)(2,1)S(1)}) fusion(s32[512]{0:T(512)S(1)} %iota_add_fusion.3), kind=kLoop, calls=%fused_computation.16.clone.1 | loop fusion | flops 18874368 | bytes 4196352 | tf_op jit(solution)/shard_map/while/body/eval_jaxpr/convert_element_type | solution.py:38
  204.9 0.6 fusion.52
  205.6 0.6 dynamic_slice.9
  206.9 17.1 %multiply_convert_fusion.5 = (bf16[2048,512]{1,0:T(8,128)(2,1)S(1)}, bf16[2048,512]{1,0:T(8,128)(2,1)S(1)}) fusion(s32[512]{0:T(512)S(1)} %iota_add_fusion.3), kind=kLoop, calls=%fused_computation.16.clone.1 | loop fusion | flops 18874368 | bytes 4196352 | tf_op jit(solution)/shard_map/while/body/eval_jaxpr/convert_element_type | solution.py:38
  224.0 0.6 fusion.52
  224.8 0.0 copy-start.3
  224.8 28.8 %scatter_custom_fusion = f32[1024]{0:T(1024)S(1)} fusion(s32[4096]{0:T(1024)S(1)} %bitcast.67, f32[4096]{0:T(1024)S(1)} %bitcast.70, f32[]{:T(128)} %constant.93.clone.1), kind=kCustom, calls=%fused_computation.77 | custom fusion | flops 4096 | bytes 4100 | tf_op jit(solution)/shard_map/scatter-add | solution.py:95
  253.6 95.0 %psum.7 = f32[1024]{0:T(1024)} all-reduce(f32[1024]{0:T(1024)S(1)} %broadcast_multiply_fusion), channel_id=1, replica_groups=mesh['gz'=16,'gy'=32] {'gz','gy'}, use_global_device_ids=true, to_apply=%region_4.5 | all-reduce | flops 1024 | bytes 8192 | tf_op jit(solution)/shard_map/psum | solution.py:98
  (32 shorter events, 0.4 us)
Async XLA Ops:
  7.2 36.9 %copy-start = (f32[3,2,64,128]{3,2,1,0:T(8,128)S(1)}, f32[3,2,64,128]{3,2,1,0:T(8,128)}, u32[]{:S(2)}) copy-start(f32[3,2,64,128]{3,2,1,0:T(8,128)} %param.7) | copy-start | bytes 589828
  7.2 36.9 %copy-start.1 = (f32[2,64,128]{2,1,0:T(8,128)S(1)}, f32[2,64,128]{2,1,0:T(8,128)}, u32[]{:S(2)}) copy-start(f32[2,64,128]{2,1,0:T(8,128)} %param.8) | copy-start | bytes 196612
  7.2 117.0 %all-gather.2.cloned.1.call-start = ((), (), s32[]{:S(2)}) async-start(), calls=%async_computation.1 | async-start | bytes 1671168 | tf_op jit(solution)/shard_map/all_gather | solution.py:67
  8.4 11.9 %collective-permute-start = (f32[3,2,64,1]{3,2,1,0:T(8,128)S(1)}, f32[3,2,64,1]{3,2,1,0:T(8,128)S(1)}, u32[]{:S(2)}, u32[]{:S(2)}) collective-permute-start(f32[3,2,64,1]{3,2,1,0:T(8,128)S(1)} %get-tuple-element.98), channel_id=1, source_target_pairs={{32,0},{64,32},{96,64},{128,96},{160,128},{192,160},{224,192},{256... | collective-permute-start | bytes 4616 | tf_op jit(solution)/shard_map/ppermute | solution.py:22
  16.8 11.0 %collective-permute-start.1 = (f32[3,2,64,1]{3,2,1,0:T(8,128)S(1)}, f32[3,2,64,1]{3,2,1,0:T(8,128)S(1)}, u32[]{:S(2)}, u32[]{:S(2)}) collective-permute-start(f32[3,2,64,1]{3,2,1,0:T(8,128)S(1)} %get-tuple-element.99), channel_id=1, source_target_pairs={{0,32},{32,64},{64,96},{96,128},{128,160},{160,192},{192,224},{224... | collective-permute-start | bytes 4616 | tf_op jit(solution)/shard_map/ppermute | solution.py:20
  28.6 6.6 %collective-permute-start.2 = (f32[3,2,1,130]{3,2,1,0:T(1,128)S(1)}, f32[3,2,1,130]{3,2,1,0:T(1,128)S(1)}, u32[]{:S(2)}, u32[]{:S(2)}) collective-permute-start(f32[3,2,1,130]{3,2,1,0:T(1,128)S(1)} %get-tuple-element.95), channel_id=1, source_target_pairs={{1,0},{2,1},{3,2},{4,3},{5,4},{6,5},{7,6},{8,7},{9,8},{10,9},{11,1... | collective-permute-start | bytes 9368 | tf_op jit(solution)/shard_map/ppermute | solution.py:22
  32.4 9.9 %collective-permute-start.3 = (f32[3,2,1,130]{3,2,1,0:T(1,128)S(1)}, f32[3,2,1,130]{3,2,1,0:T(1,128)S(1)}, u32[]{:S(2)}, u32[]{:S(2)}) collective-permute-start(f32[3,2,1,130]{3,2,1,0:T(1,128)S(1)} %get-tuple-element.96), channel_id=1, source_target_pairs={{0,1},{1,2},{2,3},{3,4},{4,5},{5,6},{6,7},{7,8},{8,9},{9,10},{10,1... | collective-permute-start | bytes 9368 | tf_op jit(solution)/shard_map/ppermute | solution.py:20
  44.8 94.3 %copy-start.2 = (s32[2,2048]{1,0:T(2,128)S(1)}, s32[2,2048]{1,0:T(2,128)}, u32[]{:S(2)}) copy-start(s32[2,2048]{1,0:T(2,128)} %param.11) | copy-start | bytes 49156
  127.2 20.5 %all-to-all-start = ((bf16[32,2,768]{2,1,0:T(2,128)(2,1)}), bf16[32,2,768]{2,1,0:T(2,128)(2,1)S(1)}, u32[]{:S(2)}, u32[]{:S(2)}) async-start(bf16[32,2,768]{2,1,0:T(2,128)(2,1)} %reshape.73), calls=%async_computation | async-start | bytes 196608 | tf_op jit(solution)/shard_map/all_to_all | solution.py:72
  224.8 123.8 %copy-start.3 = (f32[4,2,512]{2,1,0:T(2,128)}, f32[4,2,512]{2,1,0:T(2,128)S(1)}, u32[]{:S(2)}) copy-start(f32[4,2,512]{2,1,0:T(2,128)S(1)} %get-tuple-element.69) | copy-start | bytes 49156
Sparse Core Ops, SparseCore 0:
  44.9 79.1 all-gather.1
where the time goes:
time: 356 us; the launch traced here: 355 us
  other arithmetic  106 us (30%)
  waiting for transfers between devices  99.3 us (28%)
  blocking collectives  95 us (27%)
  starting transfers between devices  28 us (8%)
  between operations  14.3 us (4%)
  local copies, waits for them, and re-layouts  5.11 us (1%)
  matrix products  4.56 us (1%)
    psum x1, blocking collectives, on_device(): spectrum = lax.psum(local_bins, ('gz', 'gy'))  95 us
    all_gather x1, waiting for transfers between devices, on_device(): lax.all_gather(emf, 'gz', axis=3, tiled=True)  75.1 us
    convert_element_type x5, other arithmetic, twiddle(): (jnp.cos(angle) * factor).astype(jnp.bfloat16)  70.6 us
    scatter-add x1, other arithmetic, on_device(): jax.ops.segment_sum(mode_power.reshape(-1), bins.reshape(-1), num_segment...  28.8 us
    ppermute x2, waiting for transfers between devices, extended(): lax.ppermute(tail, axis, [(i, (i + 1) % count) for i in range(count)])  14.5 us
    ppermute x2, starting transfers between devices, extended(): lax.ppermute(head, axis, [((i + 1) % count, i) for i in range(count)])  12.2 us
    all_to_all x1, starting transfers between devices, on_device(): lax.all_to_all(z_modes, 'gy', split_axis=1, concat_axis=4, tiled=True)  11.8 us
    all_to_all x1, waiting for transfers between devices, on_device(): lax.all_to_all(z_modes, 'gy', split_axis=1, concat_axis=4, tiled=True)  8.73 us
  transfers between devices with their start and end apart: 6, of which 5 were waited for; matrix products, arithmetic and copies ran while one was open for 2% of the time, Pallas kernels for 0%

commit v1 on v0

--- a/solution.py
+++ b/solution.py
@@ -8,6 +8,13 @@
 NZ = 2048
 NB = 1024
 KZ = 1024
+
+
+def load_edges(payload):
+    inter = jnp.concatenate(
+        lax.all_to_all(jnp.stack(lax.axis_size("gz") * [payload]), "gz", 0, 0), axis=3
+    )
+    return inter
 
 
 def extended(cells, sides, width):
@@ -63,10 +70,7 @@
     z_cos, z_sin = twiddle(z_pos, k_start + jnp.arange(kz_dev, dtype=jnp.int32), NZ)
     table_z = jnp.concatenate([z_cos, -z_sin], axis=1)
     summed = jnp.einsum(
-        "cxyz,zk->kcxy",
-        lax.all_gather(emf, "gz", axis=3, tiled=True),
-        table_z,
-        preferred_element_type=jnp.float32,
+        "cxyz,zk->kcxy", load_edges(emf), table_z, preferred_element_type=jnp.float32
     )
     z_modes = summed.reshape(2, kz_dev, 3, planes, y_local).astype(jnp.bfloat16)
     spread = lax.all_to_all(z_modes, "gy", split_axis=1, concat_axis=4, tiled=True)

time: 356 us -> 307 us (0.86)
  waiting for transfers between devices: 99.3 us -> 54.3 us
  between operations: 14.3 us -> 0.92 us
  starting transfers between devices: 28 us -> 34.5 us
    all_gather x1 -> x0, waiting for transfers between devices: 75.1 us -> none  [on_device(): lax.all_gather(emf, 'gz', axis=3, tiled=True)]
    all_to_all x0 -> x1, waiting for transfers between devices: none -> 30.1 us  [load_edges(): lax.all_to_all(jnp.stack(lax.axis_size('gz') * [payload]), 'gz', 0, 0)]
    all_to_all x0 -> x1, starting transfers between devices: none -> 6.8 us  [load_edges(): lax.all_to_all(jnp.stack(lax.axis_size('gz') * [payload]), 'gz', 0, 0)]
where the time goes in v1:
time: 307 us; the launch traced here: 306 us
  other arithmetic  107 us (35%)
  blocking collectives  94.1 us (31%)
  waiting for transfers between devices  54.3 us (18%)
  starting transfers between devices  34.5 us (11%)
  local copies, waits for them, and re-layouts  8.31 us (3%)
  matrix products  4.53 us (1%)
    psum x1, blocking collectives, on_device(): spectrum = lax.psum(local_bins, ('gz', 'gy'))  94.1 us
    convert_element_type x5, other arithmetic, twiddle(): (jnp.cos(angle) * factor).astype(jnp.bfloat16)  70.6 us
    all_to_all x1, waiting for transfers between devices, load_edges(): lax.all_to_all(jnp.stack(lax.axis_size('gz') * [payload]), 'gz', 0, 0)  30.1 us
    scatter-add x1, other arithmetic, on_device(): jax.ops.segment_sum(mode_power.reshape(-1), bins.reshape(-1), num_segment...  28.8 us
    ppermute x2, waiting for transfers between devices, extended(): lax.ppermute(tail, axis, [(i, (i + 1) % count) for i in range(count)])  14.5 us
    ppermute x2, starting transfers between devices, extended(): lax.ppermute(head, axis, [((i + 1) % count, i) for i in range(count)])  12.2 us
    all_to_all x1, starting transfers between devices, on_device(): lax.all_to_all(z_modes, 'gy', split_axis=1, concat_axis=4, tiled=True)  11.5 us
    all_to_all x1, waiting for transfers between devices, on_device(): lax.all_to_all(z_modes, 'gy', split_axis=1, concat_axis=4, tiled=True)  8.73 us
  transfers between devices with their start and end apart: 6, of which 5 were waited for; matrix products, arithmetic and copies ran while one was open for 2% of the time, Pallas kernels for 0%

profile of v1, /device:TPU:1, one launch (start us, length us, event | category | flops | bytes accessed | tf_op | source)
XLA Modules:
  0.0 306.0 jit_solution(15833572891760499516)
XLA Ops:
  0.6 0.0 copy-start
  0.7 1.2 fusion.40
  1.8 8.4 %collective-permute-start = (f32[3,2,64,1]{3,2,1,0:T(8,128)S(1)}, f32[3,2,64,1]{3,2,1,0:T(8,128)S(1)}, u32[]{:S(2)}, u32[]{:S(2)}) collective-permute-start(f32[3,2,64,1]{3,2,1,0:T(8,128)S(1)} %get-tuple-element.98), channel_id=1, source_target_pairs={{32,0},{64,32},{96,64},{128,96},{160,128},{192,160},{224,192},{256... | collective-permute-start | bytes 4616 | tf_op jit(solution)/shard_map/ppermute | solution.py:29
  10.2 1.9 collective-permute-start.1
  12.2 0.7 divide_multiply_fusion
  12.8 1.0 collective-permute-done
  13.8 7.4 %collective-permute-done.1 = f32[3,2,64,1]{3,2,1,0:T(8,128)S(1)} collective-permute-done((f32[3,2,64,1]{3,2,1,0:T(8,128)S(1)}, f32[3,2,64,1]{3,2,1,0:T(8,128)S(1)}, u32[]{:S(2)}, u32[]{:S(2)}) %collective-permute-start.1) | collective-permute-done | bytes 1568 | tf_op jit(solution)/shard_map/ppermute | solution.py:27
  21.2 0.9 pad_maximum_fusion.12
  22.0 3.8 %collective-permute-start.2 = (f32[3,2,1,130]{3,2,1,0:T(1,128)S(1)}, f32[3,2,1,130]{3,2,1,0:T(1,128)S(1)}, u32[]{:S(2)}, u32[]{:S(2)}) collective-permute-start(f32[3,2,1,130]{3,2,1,0:T(1,128)S(1)} %get-tuple-element.95), channel_id=1, source_target_pairs={{1,0},{2,1},{3,2},{4,3},{5,4},{6,5},{7,6},{8,7},{9,8},{10,9},{11,1... | collective-permute-start | bytes 9368 | tf_op jit(solution)/shard_map/ppermute | solution.py:29
  25.8 2.1 collective-permute-start.3
  28.0 0.7 divide_multiply_fusion.1
  28.6 0.0 collective-permute-done.2
  28.6 7.1 %collective-permute-done.3 = f32[3,2,1,130]{3,2,1,0:T(1,128)S(1)} collective-permute-done((f32[3,2,1,130]{3,2,1,0:T(1,128)S(1)}, f32[3,2,1,130]{3,2,1,0:T(1,128)S(1)}, u32[]{:S(2)}, u32[]{:S(2)}) %collective-permute-start.3) | collective-permute-done | bytes 3152 | tf_op jit(solution)/shard_map/ppermute | solution.py:27
  35.7 1.7 fusion.29
  37.4 0.1 fusion.35
  37.5 0.0 copy-start.1
  37.5 1.5 stack.18
  39.1 6.8 %all-to-all-start = ((bf16[16,3,2,64,128]{4,3,2,1,0:T(8,128)(2,1)}), bf16[16,3,2,64,128]{4,3,2,1,0:T(8,128)(2,1)S(1)}, u32[]{:S(2)}, u32[]{:S(2)}) async-start(bf16[16,3,2,64,128]{4,3,2,1,0:T(8,128)(2,1)} %stack.18), calls=%async_computation | async-start | bytes 3145728 | tf_op jit(solution)/shard_map/all_to_all | solution.py:15
  45.9 2.1 fusion.25
  48.0 2.1 multiply_convert_fusion.3
  50.2 0.8 pad_maximum_fusion
  51.0 30.1 %all-to-all-done = bf16[16,3,2,64,128]{4,3,2,1,0:T(8,128)(2,1)S(1)} async-done(((bf16[16,3,2,64,128]{4,3,2,1,0:T(8,128)(2,1)}), bf16[16,3,2,64,128]{4,3,2,1,0:T(8,128)(2,1)S(1)}, u32[]{:S(2)}, u32[]{:S(2)}) %all-to-all-start) | async-done | bytes 1572896 | tf_op jit(solution)/shard_map/all_to_all | solution.py:15
  81.1 1.0 copy.13
  82.2 0.7 reshape.92
  82.9 0.0 copy-start.3
  82.9 1.9 convolution_convert_fusion
  84.9 0.2 copy.24
  85.1 0.8 reshape.96
  85.9 11.5 %all-to-all-start.1 = ((bf16[32,2,768]{2,1,0:T(2,128)(2,1)}), bf16[32,2,768]{2,1,0:T(2,128)(2,1)S(1)}, u32[]{:S(2)}, u32[]{:S(2)}) async-start(bf16[32,2,768]{2,1,0:T(2,128)(2,1)} %reshape.96), calls=%async_computation.1 | async-start | bytes 196608 | tf_op jit(solution)/shard_map/all_to_all | solution.py:76
  97.4 8.7 %all-to-all-done.1 = bf16[32,2,768]{2,1,0:T(2,128)(2,1)S(1)} async-done(((bf16[32,2,768]{2,1,0:T(2,128)(2,1)}), bf16[32,2,768]{2,1,0:T(2,128)(2,1)S(1)}, u32[]{:S(2)}, u32[]{:S(2)}) %all-to-all-start.1) | async-done | bytes 98336 | tf_op jit(solution)/shard_map/all_to_all | solution.py:76
  106.1 0.2 reshape.97
  106.4 0.2 reshape.79
  106.6 76.5 %while.13 = (s32[]{:T(128)}, f32[4,2,512]{2,1,0:T(2,128)S(1)}, s32[4]{0:T(128)S(1)}, bf16[24,2048]{1,0:T(8,128)(2,1)S(1)}, s32[]{:T(128)}, /*index=5*/s32[1]{0:T(128)}, f32[]{:T(128)}) while((s32[]{:T(128)}, f32[4,2,512]{2,1,0:T(2,128)S(1)}, s32[4]{0:T(128)S(1)}, bf16[24,2048]{1,0:T(8,128)(2,1)S(1)}, s32[]{:T(128)}, ...), condition=%wide.region_2.3_spmd.clone, body=%wide.region_0.2_spmd.clone.sunk | while | flops 127963648 | bytes 8798321 | solution.py:97
  106.6 0.6 dynamic_slice.9
  107.9 17.1 %multiply_convert_fusion.5 = (bf16[2048,512]{1,0:T(8,128)(2,1)S(1)}, bf16[2048,512]{1,0:T(8,128)(2,1)S(1)}) fusion(s32[512]{0:T(512)S(1)} %iota_add_fusion.3), kind=kLoop, calls=%fused_computation.16.clone.1 | loop fusion | flops 18874368 | bytes 4196352 | tf_op jit(solution)/shard_map/while/body/eval_jaxpr/convert_element_type | solution.py:45
  125.0 0.6 fusion.50
  125.7 0.6 dynamic_slice.9
  127.0 17.1 %multiply_convert_fusion.5 = (bf16[2048,512]{1,0:T(8,128)(2,1)S(1)}, bf16[2048,512]{1,0:T(8,128)(2,1)S(1)}) fusion(s32[512]{0:T(512)S(1)} %iota_add_fusion.3), kind=kLoop, calls=%fused_computation.16.clone.1 | loop fusion | flops 18874368 | bytes 4196352 | tf_op jit(solution)/shard_map/while/body/eval_jaxpr/convert_element_type | solution.py:45
  144.1 0.6 fusion.50
  144.9 0.6 dynamic_slice.9
  146.1 17.1 %multiply_convert_fusion.5 = (bf16[2048,512]{1,0:T(8,128)(2,1)S(1)}, bf16[2048,512]{1,0:T(8,128)(2,1)S(1)}) fusion(s32[512]{0:T(512)S(1)} %iota_add_fusion.3), kind=kLoop, calls=%fused_computation.16.clone.1 | loop fusion | flops 18874368 | bytes 4196352 | tf_op jit(solution)/shard_map/while/body/eval_jaxpr/convert_element_type | solution.py:45
  163.2 0.6 fusion.50
  164.0 0.6 dynamic_slice.9
  165.2 17.1 %multiply_convert_fusion.5 = (bf16[2048,512]{1,0:T(8,128)(2,1)S(1)}, bf16[2048,512]{1,0:T(8,128)(2,1)S(1)}) fusion(s32[512]{0:T(512)S(1)} %iota_add_fusion.3), kind=kLoop, calls=%fused_computation.16.clone.1 | loop fusion | flops 18874368 | bytes 4196352 | tf_op jit(solution)/shard_map/while/body/eval_jaxpr/convert_element_type | solution.py:45
  182.4 0.6 fusion.50
  183.1 0.0 copy-start.4
  183.2 28.8 %scatter_custom_fusion = f32[1024]{0:T(1024)S(1)} fusion(s32[4096]{0:T(1024)S(1)} %bitcast.74, f32[4096]{0:T(1024)S(1)} %bitcast.77, f32[]{:T(128)} %constant.93.clone.1), kind=kCustom, calls=%fused_computation.75 | custom fusion | flops 4096 | bytes 4100 | tf_op jit(solution)/shard_map/scatter-add | solution.py:99
  212.0 94.1 %psum.7 = f32[1024]{0:T(1024)} all-reduce(f32[1024]{0:T(1024)S(1)} %broadcast_multiply_fusion), channel_id=1, replica_groups=mesh['gz'=16,'gy'=32] {'gz','gy'}, use_global_device_ids=true, to_apply=%region_4.5 | all-reduce | flops 1024 | bytes 8192 | tf_op jit(solution)/shard_map/psum | solution.py:102
  (35 shorter events, 0.4 us)
Async XLA Ops:
  0.6 36.8 %copy-start = (f32[3,2,64,128]{3,2,1,0:T(8,128)S(1)}, f32[3,2,64,128]{3,2,1,0:T(8,128)}, u32[]{:S(2)}) copy-start(f32[3,2,64,128]{3,2,1,0:T(8,128)} %param.7) | copy-start | bytes 589828
  0.6 36.8 %copy-start.2 = (f32[2,64,128]{2,1,0:T(8,128)S(1)}, f32[2,64,128]{2,1,0:T(8,128)}, u32[]{:S(2)}) copy-start(f32[2,64,128]{2,1,0:T(8,128)} %param.8) | copy-start | bytes 196612
  1.8 11.9 %collective-permute-start = (f32[3,2,64,1]{3,2,1,0:T(8,128)S(1)}, f32[3,2,64,1]{3,2,1,0:T(8,128)S(1)}, u32[]{:S(2)}, u32[]{:S(2)}) collective-permute-start(f32[3,2,64,1]{3,2,1,0:T(8,128)S(1)} %get-tuple-element.98), channel_id=1, source_target_pairs={{32,0},{64,32},{96,64},{128,96},{160,128},{192,160},{224,192},{256... | collective-permute-start | bytes 4616 | tf_op jit(solution)/shard_map/ppermute | solution.py:29
  10.2 11.0 %collective-permute-start.1 = (f32[3,2,64,1]{3,2,1,0:T(8,128)S(1)}, f32[3,2,64,1]{3,2,1,0:T(8,128)S(1)}, u32[]{:S(2)}, u32[]{:S(2)}) collective-permute-start(f32[3,2,64,1]{3,2,1,0:T(8,128)S(1)} %get-tuple-element.99), channel_id=1, source_target_pairs={{0,32},{32,64},{64,96},{96,128},{128,160},{160,192},{192,224},{224... | collective-permute-start | bytes 4616 | tf_op jit(solution)/shard_map/ppermute | solution.py:27
  22.0 6.6 %collective-permute-start.2 = (f32[3,2,1,130]{3,2,1,0:T(1,128)S(1)}, f32[3,2,1,130]{3,2,1,0:T(1,128)S(1)}, u32[]{:S(2)}, u32[]{:S(2)}) collective-permute-start(f32[3,2,1,130]{3,2,1,0:T(1,128)S(1)} %get-tuple-element.95), channel_id=1, source_target_pairs={{1,0},{2,1},{3,2},{4,3},{5,4},{6,5},{7,6},{8,7},{9,8},{10,9},{11,1... | collective-permute-start | bytes 9368 | tf_op jit(solution)/shard_map/ppermute | solution.py:29
  25.8 9.9 %collective-permute-start.3 = (f32[3,2,1,130]{3,2,1,0:T(1,128)S(1)}, f32[3,2,1,130]{3,2,1,0:T(1,128)S(1)}, u32[]{:S(2)}, u32[]{:S(2)}) collective-permute-start(f32[3,2,1,130]{3,2,1,0:T(1,128)S(1)} %get-tuple-element.96), channel_id=1, source_target_pairs={{0,1},{1,2},{2,3},{3,4},{4,5},{5,6},{6,7},{7,8},{8,9},{9,10},{10,1... | collective-permute-start | bytes 9368 | tf_op jit(solution)/shard_map/ppermute | solution.py:27
  37.5 1.6 copy-start.1
  39.1 42.1 %all-to-all-start = ((bf16[16,3,2,64,128]{4,3,2,1,0:T(8,128)(2,1)}), bf16[16,3,2,64,128]{4,3,2,1,0:T(8,128)(2,1)S(1)}, u32[]{:S(2)}, u32[]{:S(2)}) async-start(bf16[16,3,2,64,128]{4,3,2,1,0:T(8,128)(2,1)} %stack.18), calls=%async_computation | async-start | bytes 3145728 | tf_op jit(solution)/shard_map/all_to_all | solution.py:15
  82.9 14.5 %copy-start.3 = (s32[2,2048]{1,0:T(2,128)S(1)}, s32[2,2048]{1,0:T(2,128)}, u32[]{:S(2)}) copy-start(s32[2,2048]{1,0:T(2,128)} %param.11) | copy-start | bytes 49156
  85.9 20.3 %all-to-all-start.1 = ((bf16[32,2,768]{2,1,0:T(2,128)(2,1)}), bf16[32,2,768]{2,1,0:T(2,128)(2,1)S(1)}, u32[]{:S(2)}, u32[]{:S(2)}) async-start(bf16[32,2,768]{2,1,0:T(2,128)(2,1)} %reshape.96), calls=%async_computation.1 | async-start | bytes 196608 | tf_op jit(solution)/shard_map/all_to_all | solution.py:76
  183.1 122.9 %copy-start.4 = (f32[4,2,512]{2,1,0:T(2,128)}, f32[4,2,512]{2,1,0:T(2,128)S(1)}, u32[]{:S(2)}) copy-start(f32[4,2,512]{2,1,0:T(2,128)S(1)} %get-tuple-element.69) | copy-start | bytes 49156
